TPU v7x, 256 devices: a whole 4x4x8 slice. The times are simulated.
256 devices in a mesh: row: 16 (over y, x), col: 16 (over z, core).
Axes of the slice: x: 4, y: 4, z: 8, core: 2. Of those that a mesh axis runs over, the one named last changes fastest.
Arguments:
- trailing: float32 [8192, 8192], P('row', 'col'), may hold values from -6 to 6
- panel_block: float32 [8192, 512], P('row'), may hold values from -1 to 1
Outputs:
- updated: float32 [8192, 8192], P('row', 'col')
- band_block: float32 [512, 512], replicated
All inputs are finite; a program needn't handle non-finite values.
Results may differ from a plain program's by a relative error of at most 0.00015.
Values sent between devices are 32-bit elements; how exact they have to be, the bound alone decides.
A program may use at most 64 MiB of HBM per device.

v0:
```python
import jax
import jax.numpy as jnp
from jax import lax
from jax.sharding import Mesh
from jax.sharding import PartitionSpec as P

COL = ("col_0", "col_1")


PRECISE = lax.Precision.HIGHEST


def rows_for(lines, count):
    spare = -lines.shape[0] % count
    if not spare:
        return lines
    return jnp.concatenate([lines, jnp.zeros((spare, *lines.shape[1:]), lines.dtype)])


def spread(array, axis, root):
    lines = jnp.where(lax.axis_index(axis) == root, array, jnp.zeros_like(array)).reshape(
        -1, *array.shape[1:][-1:]
    )
    padded = rows_for(lines, lax.axis_size(axis))
    own = lax.psum_scatter(padded, axis, scatter_dimension=0, tiled=True)
    return lax.all_gather(own, axis, axis=0, tiled=True)[: len(lines)].reshape(array.shape)


def own_block(parts, axes, order):
    inside = parts.shape[1:]
    parts = parts.reshape(*(lax.axis_size(a) for a in axes), *inside)
    parts = jnp.moveaxis(parts, order, range(len(axes))).reshape(-1, *inside)
    for k in order:
        parts = lax.psum_scatter(parts, axes[k], scatter_dimension=0, tiled=True)
    return parts[0]


def all_blocks(array, axes, order):
    parts = array
    for k in order:
        parts = lax.all_gather(parts, axes[k])
    done = order[::-1]
    back = [done.index(k) for k in range(len(axes))]
    parts = parts.transpose(*back, *range(len(axes), parts.ndim))
    return parts.reshape(-1, *array.shape)


def sum_in_two_steps(array, axes, order):
    count, lines = (lax.axis_size(axes), array.reshape(-1, *array.shape[1:][-1:]))
    parts = rows_for(lines, count).reshape(count, -1, *lines.shape[1:])
    own = own_block(parts, axes, order)
    whole = all_blocks(own, axes, order[::-1]).reshape(-1, *lines.shape[1:])
    return whole[: len(lines)].reshape(array.shape)


def spread_2(value, axis, source):
    kept = jnp.where(lax.axis_index(axis) == source, value, 0).astype(value.dtype)
    return lax.psum(kept, axis)


def product(former, latter):
    return jnp.dot(former, latter, precision=PRECISE, preferred_element_type=jnp.float32)


def cross_gram(former, latter):
    return lax.dot_general(
        former,
        latter,
        (((0,), (0,)), ((), ())),
        precision=PRECISE,
        preferred_element_type=jnp.float32,
    )


def local(trailing, panel_block):
    rows_dev, cols_dev = trailing.shape
    band_width = panel_block.shape[1]
    row_index = lax.axis_index("row")
    col_index = lax.axis_index(COL)
    col_per_row = lax.axis_size(COL) // lax.axis_size("row")
    identity = jnp.eye(band_width, dtype=jnp.float32)
    leading = panel_block * (row_index == 0).astype(jnp.float32)
    gram_local = cross_gram(panel_block, panel_block)
    gram_total, leading_total = lax.psum((gram_local, leading), "row")
    lower_factor = jnp.linalg.cholesky(gram_total)
    orthonormal = jax.scipy.linalg.solve_triangular(lower_factor, panel_block.T, lower=True).T
    basis_top = jax.scipy.linalg.solve_triangular(lower_factor, leading_total.T, lower=True).T
    system = identity + basis_top.T
    factor_square = jnp.linalg.cholesky(product(system, system.T))
    inverse = product(system.T, jax.scipy.linalg.cho_solve((factor_square, True), identity))
    row_ids = lax.broadcasted_iota(jnp.int32, (rows_dev, band_width), 0) + row_index * rows_dev
    col_ids = lax.broadcasted_iota(jnp.int32, (rows_dev, band_width), 1)
    reflector = orthonormal + (row_ids == col_ids).astype(jnp.float32)
    owner_row = col_index // col_per_row
    offset = col_index % col_per_row * cols_dev
    reflector_cols = spread(reflector, "row", owner_row)
    partial_value = product(trailing, product(reflector_cols, inverse))
    applied = sum_in_two_steps(partial_value, COL, (0, 1))
    coupled = lax.psum(cross_gram(reflector, applied), "row")
    coupling = product(inverse.T, coupled)
    correct_rows = applied - 0.5 * product(reflector, coupling)
    correct_cols = spread_2(correct_rows, "row", owner_row)
    left_side = jnp.concatenate([reflector, correct_rows], axis=1)
    right_side = jnp.concatenate([correct_cols, reflector_cols], axis=1)
    updated = trailing - lax.dot_general(
        left_side,
        right_side,
        (((1,), (1,)), ((), ())),
        precision=PRECISE,
        preferred_element_type=jnp.float32,
    )
    return (updated, -lower_factor.T)


def solution(mesh):
    finer = Mesh(mesh.devices.reshape(mesh.shape["row"], 8, 2), ("row", "col_0", "col_1"))
    placed = (P("row", COL), P("row", None))
    return jax.shard_map(
        local, mesh=finer, in_specs=placed, out_specs=(P("row", COL), P()), check_vma=False
    )
```

profile of v0, /device:TPU:32, one launch (start us, length us, event | category | flops | bytes accessed | tf_op | source)
XLA Modules:
  0.0 801.7 jit_solution(17051203057399958474)
XLA Ops:
  7.2 4.5 fusion.127
  14.3 102.6 %all-reduce.10.cloned.1.call-done = (f32[512,512]{0,1:T(8,128)}, f32[512,512]{0,1:T(8,128)}) async-done(((f32[512,512]{0,1:T(8,128)}, f32[512,512]{0,1:T(8,128)}), (f32[512,512]{0,1:T(8,128)}, f32[512,512]{0,1:T(8,128)})) %all-reduce.10.cloned.1.call-update) | async-done | bytes 2097168 | tf_op jit(solution)/shard_map/psum | solution.py:84
  116.9 1.6 copy.14
  119.8 11.7 %cholesky.286 = f32[128,128]{1,0:T(8,128)S(1)} custom-call(f32[128,128]{1,0:T(8,128)S(1)} %cholesky.426), custom_call_target="Cholesky" | custom-call | tf_op jit(solution)/shard_map/jit(cholesky)/cholesky | solution.py:85
  131.5 9.8 %custom-call.33 = f32[1,128,128]{1,2,0:T(8,128)S(1)} custom-call(f32[1,128,128]{2,1,0:T(8,128)S(1)} %get-tuple-element.84), custom_call_target="InvertDiagBlocksLowerTriangular" | custom-call | tf_op jit(solution)/shard_map/jit(cholesky)/cholesky | solution.py:85
  142.8 11.7 %cholesky.305 = f32[128,128]{1,0:T(8,128)S(1)} custom-call(f32[128,128]{1,0:T(8,128)S(1)} %cholesky.430), custom_call_target="Cholesky" | custom-call | tf_op jit(solution)/shard_map/jit(cholesky)/cholesky | solution.py:85
  154.6 10.2 %custom-call.34 = f32[1,128,128]{1,2,0:T(8,128)S(1)} custom-call(f32[1,128,128]{2,1,0:T(8,128)S(1)} %get-tuple-element.81), custom_call_target="InvertDiagBlocksLowerTriangular" | custom-call | tf_op jit(solution)/shard_map/jit(cholesky)/cholesky | solution.py:85
  166.4 11.7 %cholesky.326 = f32[128,128]{1,0:T(8,128)S(1)} custom-call(f32[128,128]{1,0:T(8,128)S(1)} %cholesky.435), custom_call_target="Cholesky" | custom-call | tf_op jit(solution)/shard_map/jit(cholesky)/cholesky | solution.py:85
  178.8 9.8 %custom-call.35 = f32[1,128,128]{1,2,0:T(8,128)S(1)} custom-call(f32[1,128,128]{2,1,0:T(8,128)S(1)} %get-tuple-element.78), custom_call_target="InvertDiagBlocksLowerTriangular" | custom-call | tf_op jit(solution)/shard_map/jit(cholesky)/cholesky | solution.py:85
  189.2 11.7 %cholesky.343 = f32[128,128]{1,0:T(8,128)S(1)} custom-call(f32[128,128]{1,0:T(8,128)S(1)} %convolution_subtract_fusion.17), custom_call_target="Cholesky" | custom-call | tf_op jit(solution)/shard_map/jit(cholesky)/cholesky | solution.py:85
  206.2 7.9 while.8
  206.8 1.4 bitcast_dynamic-update-slice_fusion.5
  208.8 1.4 bitcast_dynamic-update-slice_fusion.5
  210.8 1.4 bitcast_dynamic-update-slice_fusion.5
  212.8 1.4 bitcast_dynamic-update-slice_fusion.5
  214.1 39.3 %custom-call.36 = f32[4,128,128]{1,2,0:T(8,128)S(1)} custom-call(f32[4,128,128]{2,1,0:T(8,128)S(1)} %get-tuple-element.32), custom_call_target="InvertDiagBlocksLowerTriangular" | custom-call | tf_op jit(solution)/shard_map/jit(_solve_triangular)/triangular_solve/custom-call.1 | solution.py:86
  256.3 2.2 convolution_subtract_fusion.11
  263.9 1.5 convolution_subtract_fusion.10
  266.6 1.8 fusion.59
  269.0 12.1 %cholesky.358 = f32[128,128]{1,0:T(8,128)S(1)} custom-call(f32[128,128]{1,0:T(8,128)S(1)} %cholesky.439), custom_call_target="Cholesky" | custom-call | tf_op jit(solution)/shard_map/jit(cholesky)/cholesky | solution.py:89
  281.3 9.8 %custom-call.38 = f32[1,128,128]{1,2,0:T(8,128)S(1)} custom-call(f32[1,128,128]{2,1,0:T(8,128)S(1)} %get-tuple-element.74), custom_call_target="InvertDiagBlocksLowerTriangular" | custom-call | tf_op jit(solution)/shard_map/jit(cholesky)/cholesky | solution.py:89
  291.8 11.7 %cholesky.377 = f32[128,128]{1,0:T(8,128)S(1)} custom-call(f32[128,128]{1,0:T(8,128)S(1)} %cholesky.443), custom_call_target="Cholesky" | custom-call | tf_op jit(solution)/shard_map/jit(cholesky)/cholesky | solution.py:89
  304.9 9.8 %custom-call.39 = f32[1,128,128]{1,2,0:T(8,128)S(1)} custom-call(f32[1,128,128]{2,1,0:T(8,128)S(1)} %get-tuple-element.71), custom_call_target="InvertDiagBlocksLowerTriangular" | custom-call | tf_op jit(solution)/shard_map/jit(cholesky)/cholesky | solution.py:89
  315.4 11.9 %cholesky.398 = f32[128,128]{1,0:T(8,128)S(1)} custom-call(f32[128,128]{1,0:T(8,128)S(1)} %cholesky.448), custom_call_target="Cholesky" | custom-call | tf_op jit(solution)/shard_map/jit(cholesky)/cholesky | solution.py:89
  328.0 9.8 %custom-call.40 = f32[1,128,128]{1,2,0:T(8,128)S(1)} custom-call(f32[1,128,128]{2,1,0:T(8,128)S(1)} %get-tuple-element.68), custom_call_target="InvertDiagBlocksLowerTriangular" | custom-call | tf_op jit(solution)/shard_map/jit(cholesky)/cholesky | solution.py:89
  338.4 11.7 %cholesky.415 = f32[128,128]{1,0:T(8,128)S(1)} custom-call(f32[128,128]{1,0:T(8,128)S(1)} %convolution_subtract_fusion.16), custom_call_target="Cholesky" | custom-call | tf_op jit(solution)/shard_map/jit(cholesky)/cholesky | solution.py:89
  352.1 2.3 broadcast_select_fusion.1
  357.2 8.4 %while.7 = (s32[]{:T(128)}, f32[512,512]{1,0:T(8,128)S(1)}, s32[4,2]{0,1:T(2,128)S(1)}, f32[4,128,128]{2,1,0:T(8,128)S(1)}, s32[]{:T(128)}) while((s32[]{:T(128)}, f32[512,512]{1,0:T(8,128)S(1)}, s32[4,2]{0,1:T(2,128)S(1)}, f32[4,128,128]{2,1,0:T(8,128)S(1)}, s32[]{:T(128)}) %tuple.89), condition=%wide.while_cond.1, body=%wide.while_body.1.sunk | while | flops 2 | bytes 131181 | solution.py:90
  365.6 39.3 %custom-call.27 = f32[4,128,128]{1,2,0:T(8,128)S(1)} custom-call(f32[4,128,128]{2,1,0:T(8,128)S(1)} %get-tuple-element.19), custom_call_target="InvertDiagBlocksLowerTriangular" | custom-call | tf_op jit(solution)/shard_map/jit(_cho_solve)/triangular_solve | solution.py:90
  404.9 1.5 fusion.60
  408.1 1.4 convolution_subtract_fusion.2
  409.9 2.3 convolution_subtract_fusion.9
  412.3 21.2 %reduce-scatter.4.cloned.1.call-done = f32[32,512]{1,0:T(8,128)} async-done(((f32[512,512]{1,0:T(8,128)}), f32[32,512]{1,0:T(8,128)}) %reduce-scatter.4.cloned.1.call-update) | async-done | bytes 65552 | tf_op jit(solution)/shard_map/reduce_scatter | solution.py:25
  433.5 1.4 fusion.109
  438.9 1.9 fusion.9
  440.8 42.0 %all-gather.4.cloned.1.call-done = f32[512,512]{1,0:T(8,128)} async-done(((f32[32,512]{1,0:T(8,128)}), f32[512,512]{1,0:T(8,128)}) %all-gather.4.cloned.1.call-update) | async-done | bytes 1048592 | tf_op jit(solution)/shard_map/all_gather | solution.py:26
  482.8 3.1 fusion.128
  485.9 2.8 fusion.129
  488.8 37.9 %reduce-scatter.6.cloned.1.call-done = f32[2,32,512]{2,1,0:T(8,128)} async-done(((f32[16,32,512]{2,1,0:T(8,128)}), f32[2,32,512]{2,1,0:T(8,128)}) %reduce-scatter.6.cloned.1.call-update) | async-done | bytes 131088 | tf_op jit(solution)/shard_map/reduce_scatter | solution.py:34
  526.8 14.4 %reduce-scatter.8.cloned.1.call-done = f32[1,32,512]{2,1,0:T(8,128)} async-done(((f32[2,32,512]{2,1,0:T(8,128)}), f32[1,32,512]{2,1,0:T(8,128)}) %reduce-scatter.8.cloned.1.call-update) | async-done | bytes 65552 | tf_op jit(solution)/shard_map/reduce_scatter | solution.py:34
  541.2 3.5 all_gather.13
  544.8 39.2 %all-gather.6.cloned.1.call-done = f32[16,32,512]{2,1,0:T(8,128)} async-done(((f32[2,32,512]{2,1,0:T(8,128)}), f32[16,32,512]{2,1,0:T(8,128)}) %all-gather.6.cloned.1.call-update) | async-done | bytes 1048592 | tf_op jit(solution)/shard_map/all_gather | solution.py:41
  584.0 4.0 fusion.130
  588.4 96.4 %all-reduce.6.cloned.1.call-done = f32[512,512]{1,0:T(8,128)} async-done(((f32[512,512]{1,0:T(8,128)}), f32[512,512]{1,0:T(8,128)}) %all-reduce.6.cloned.1.call-update) | async-done | bytes 1048592 | tf_op jit(solution)/shard_map/psum | solution.py:99
  684.7 3.2 fusion.131
  687.9 3.2 broadcast_select_fusion
  693.7 94.4 %all-reduce.8.cloned.1.call-done = f32[512,512]{1,0:T(8,128)} async-done(((f32[512,512]{1,0:T(8,128)}), f32[512,512]{1,0:T(8,128)}) %all-reduce.8.cloned.1.call-update) | async-done | bytes 1048592 | tf_op jit(solution)/shard_map/psum | solution.py:58
  788.0 6.3 fusion.22
  (147 shorter events, 46.7 us)
Async XLA Ops:
  7.2 109.7 %all-reduce.10.cloned.1.call-start = ((), (), s32[]{:S(2)}) async-start(), calls=%async_computation.10 | async-start | bytes 4194304 | tf_op jit(solution)/shard_map/psum | solution.py:84
  7.2 4.5 copy-start
  12.8 420.6 %reduce-scatter.4.cloned.1.call-start = ((), (), s32[]{:S(2)}) async-start(), calls=%async_computation.3 | async-start | bytes 1114112 | tf_op jit(solution)/shard_map/reduce_scatter | solution.py:25
  116.9 1.7 copy-start.1
  118.8 1.0 copy-start.5
  119.8 21.7 %copy-start.6 = (f32[512,512]{1,0:T(8,128)S(1)}, f32[512,512]{1,0:T(8,128)}, u32[]{:S(2)}) copy-start(f32[512,512]{1,0:T(8,128)} %copy-done.5) | copy-start | bytes 3145732
  142.1 0.7 copy-start.16
  253.4 12.0 %copy-start.9 = (f32[4,128,128]{1,2,0:T(8,128)}, f32[4,128,128]{1,2,0:T(8,128)S(1)}, u32[]{:S(2)}) copy-start(f32[4,128,128]{1,2,0:T(8,128)S(1)} %custom-call.36) | copy-start | bytes 786436
  258.5 2.5 copy-start.12
  262.5 3.4 copy-start.7
  263.9 1.9 copy-start.13
  265.9 0.7 copy-start.17
  303.5 47.4 %copy-start.15 = (f32[128,512]{0,1:T(8,128)S(1)}, f32[128,512]{0,1:T(8,128)}, u32[]{:S(2)}) copy-start(f32[128,512]{0,1:T(8,128)} %convolution_subtract_fusion.11) | copy-start | bytes 786436
  354.4 128.4 %all-gather.4.cloned.1.call-start = ((), (), s32[]{:S(2)}) async-start(), calls=%async_computation.4 | async-start | bytes 1114112 | tf_op jit(solution)/shard_map/all_gather | solution.py:26
  404.9 28.6 %copy-start.10 = (f32[4,128,128]{1,2,0:T(8,128)}, f32[4,128,128]{1,2,0:T(8,128)S(1)}, u32[]{:S(2)}) copy-start(f32[4,128,128]{1,2,0:T(8,128)S(1)} %custom-call.27) | copy-start | bytes 786436
  433.5 93.2 %reduce-scatter.6.cloned.1.call-start = ((), (), s32[]{:S(2)}) async-start(), calls=%async_computation.5 | async-start | bytes 1179648 | tf_op jit(solution)/shard_map/reduce_scatter | solution.py:34
  434.9 1.7 copy-start.11
  437.8 1.1 copy-start.8
  437.8 1.1 copy-start.14
  437.8 1.1 copy-start.18
  440.8 45.1 %copy-start.2 = (f32[512,512]{1,0:T(8,128)S(1)}, f32[512,512]{1,0:T(8,128)}, u32[]{:S(2)}) copy-start(f32[512,512]{1,0:T(8,128)} %param.5) | copy-start | bytes 3145732
  488.8 52.4 %reduce-scatter.8.cloned.1.call-start = ((), (), s32[]{:S(2)}) async-start(), calls=%async_computation.6 | async-start | bytes 196608 | tf_op jit(solution)/shard_map/reduce_scatter | solution.py:34
  526.7 57.3 %all-gather.6.cloned.1.call-start = ((), (), s32[]{:S(2)}) async-start(), calls=%async_computation.9 | async-start | bytes 1179648 | tf_op jit(solution)/shard_map/all_gather | solution.py:41
  544.8 140.0 %all-reduce.6.cloned.1.call-start = ((), (), s32[]{:S(2)}) async-start(), calls=%async_computation.7 | async-start | bytes 2097152 | tf_op jit(solution)/shard_map/psum | solution.py:99
  588.1 200.0 %all-reduce.8.cloned.1.call-start = ((), (), s32[]{:S(2)}) async-start(), calls=%async_computation.8 | async-start | bytes 2097152 | tf_op jit(solution)/shard_map/psum | solution.py:58
  684.7 3.2 copy-start.4
  691.1 1.2 copy-start.3
Sparse Core Ops, SparseCore 0:
  13.0 103.8 all-reduce.9
  354.5 78.8 reduce-scatter.3
  435.9 46.9 all-gather.3
  488.9 37.7 reduce-scatter.5
  529.0 12.1 reduce-scatter.7
  544.9 39.0 all-gather.5
  588.2 96.5 all-reduce.5
  691.3 96.7 all-reduce.7
where the time goes:
time: 805 us; the launch traced here: 802 us
  waiting for transfers between devices  448 us (56%)
  other arithmetic  244 us (30%)
  matrix products  59.1 us (7%)
  local copies, waits for them, and re-layouts  25.6 us (3%)
  between operations  20.4 us (3%)
    psum x1, waiting for transfers between devices, local(): gram_total, leading_total = lax.psum((gram_local, leading), 'row')  103 us
    psum x1, waiting for transfers between devices, local(): coupled = lax.psum(cross_gram(reflector, applied), 'row')  96.4 us
    psum x1, waiting for transfers between devices, spread_2(): return lax.psum(kept, axis)  94.4 us
    another operation x15, other arithmetic, local(): factor_square = jnp.linalg.cholesky(product(system, system.T))  79.7 us
    another operation x14, other arithmetic, local(): lower_factor = jnp.linalg.cholesky(gram_total)  79 us
    reduce_scatter x2, waiting for transfers between devices, own_block(): parts = lax.psum_scatter(parts, axes[k], scatter_dimension=0, tiled=True)  52.3 us
    all_gather x1, waiting for transfers between devices, spread(): lax.all_gather(own, axis, axis=0, tiled=True)[:len(lines)]  42 us
    another operation x2, other arithmetic, local(): jax.scipy.linalg.cho_solve((factor_square, True), identity)  39.4 us
  transfers between devices with their start and end apart: 8, of which 8 were waited for; matrix products, arithmetic and copies ran while one was open for 8% of the time, Pallas kernels for 0%

commit v1 on v0

v1 whole, which is shorter than its diff:
```python
import functools
import jax
import jax.numpy as jnp
from jax import lax
from jax.experimental import pallas as pl
from jax.experimental.pallas import tpu as pltpu
from jax.sharding import PartitionSpec as P

HI = lax.Precision.HIGHEST
F32 = jnp.float32
BF16 = jnp.bfloat16
MESH = pl.DeviceIdType.MESH
G, P0, B0, F0, R = range(5)


def dotg(a, b, ca, cb):
    return lax.dot_general(
        a, b, (((ca,), (cb,)), ((), ())), precision=HI, preferred_element_type=F32
    )


def split(x):
    high = x.astype(BF16)
    return high, (x - high.astype(F32)).astype(BF16)


def dot3(a, b, ca, cb):
    ah, al = a if isinstance(a, tuple) else split(a)
    bh, bl = b if isinstance(b, tuple) else split(b)
    dims = (((ca,), (cb,)), ((), ()))
    d = functools.partial(lax.dot_general, dimension_numbers=dims, preferred_element_type=F32)
    return d(ah, bh) + (d(ah, bl) + d(al, bh))


def bc(x):
    return jnp.broadcast_to(x, (8, 128))


def leaf(d):
    sub = lax.broadcasted_iota(jnp.int32, (8, 128), 0)
    lane = lax.broadcasted_iota(jnp.int32, (8, 128), 1)
    d = list(d)
    inv = [(lane == sub + 8 * q).astype(F32) for q in range(16)]
    upper, lower_inv = [], []
    for q in range(16):
        cb = [bc(d[q][:, 8 * q + j : 8 * q + j + 1]) for j in range(8)]
        mul = [[bc(d[p][:, 8 * q + j : 8 * q + j + 1]) for j in range(8)] for p in range(q + 1, 16)]
        zd, zi = d[q], inv[q]
        ud = jnp.zeros((8, 128), F32)
        ui = ud
        for j in range(8):
            pivot = bc(cb[j][j : j + 1, :])
            r = 1.0 / pivot
            rs = lax.rsqrt(pivot)
            rd, ri = bc(zd[j : j + 1, :]), bc(zi[j : j + 1, :])
            mine = sub == j
            ud, ui = jnp.where(mine, rd * rs, ud), jnp.where(mine, ri * rs, ui)
            pd, pi = rd * r, ri * r
            zd = jnp.where(mine, pd, zd - cb[j] * pd)
            zi = jnp.where(mine, pi, zi - cb[j] * pi)
            for k in range(j + 1, 8):
                t = bc(cb[k][j : j + 1, :]) * r
                cb[k] = jnp.where(mine, t, cb[k] - cb[j] * t)
        upper.append(jnp.where(lane >= sub + 8 * q, ud, 0.0))
        lower_inv.append(ui)
        zds = [bc(zd[j : j + 1, :]) for j in range(8)]
        zis = [bc(zi[j : j + 1, :]) for j in range(8)]
        for p in range(q + 1, 16):
            m = mul[p - q - 1]
            x, y = d[p], inv[p]
            for j in range(8):
                x, y = x - m[j] * zds[j], y - m[j] * zis[j]
            d[p], inv[p] = x, y
    return upper, lower_inv


def factor_block(b, w, u, li):
    s, e = 128 * b, 128 * b + 128
    upper, lower_inv = leaf([w[s + 8 * q : s + 8 * q + 8, s:e] for q in range(16)])
    for q in range(16):
        u[s + 8 * q : s + 8 * q + 8, s:e] = upper[q]
        li[s + 8 * q : s + 8 * q + 8, s:e] = lower_inv[q]
    lb = li[s:e, s:e]
    if b < 3:
        u[s:e, e:] = dotg(lb, w[s:e, e:], 1, 0)
    if b > 0:
        li[s:e, :s] = dotg(lb, li[s:e, :s], 1, 0)
    if b < 3:
        ut = u[s:e, e:]
        w[e:, e:] -= dotg(ut, ut, 0, 0)
        li[e:, :e] -= dotg(ut, li[s:e, :e], 0, 0)


def factor_kernel(g, nu, li, w, u):
    w[...] = g[...].reshape(512, 512)
    u[...] = jnp.zeros((512, 512), F32)
    li[...] = jnp.zeros((512, 512), F32)
    for b in range(4):
        factor_block(b, w, u, li)
    nu[...] = -u[...]


def comm_kernel(
    n, a, p, cm, pc, bct, a0c, br, fr,
    gp, bp, grs, brs, rp, rrs, bq, bsw, bsum, bz, send, recv,
):
    hs, zc = 256 // n, n // 2
    zs, ps = 256 // zc, 128 // n
    r, c = lax.axis_index("row"), lax.axis_index("col")
    z, k = lax.div(c, 2), lax.rem(c, 2)
    partner = c + 1 - 2 * k
    sent = []

    def at(i, size):
        return pl.ds(pl.multiple_of(i * size, size), size)

    def copy(src, dst, s, axis, index):
        return pltpu.make_async_remote_copy(
            src_ref=src, dst_ref=dst, send_sem=send.at[s], recv_sem=recv.at[s],
            device_id={axis: index}, device_id_type=MESH,
        )

    def wait(ref, s, sems=recv):
        pltpu.make_async_copy(ref, ref, sems.at[s]).wait()

    rows = [lax.rem(r + j, n) for j in range(1, n)]
    cols = [lax.rem(c + j, n) for j in range(1, n)]
    cores = [lax.rem(c + 2 * j, n) for j in range(1, zc)]

    barrier = pltpu.get_barrier_semaphore()
    for i in rows:
        pl.semaphore_signal(barrier, inc=1, device_id={"row": i}, device_id_type=MESH)
    for i in cols:
        pl.semaphore_signal(barrier, inc=1, device_id={"col": i}, device_id_type=MESH)
    pl.semaphore_wait(barrier, 2 * n - 2)

    PC_S, A0_S, P0_S, FR_S, G_RS, B_RS, PC_AG, A0_AG, BC_AG, CM_AG = range(10)
    CM_SW, B0_S, F0_S, R_RS, R_B, BQ_SW, B_Z, BR_AG, BR_SW, FR_AG, FR_SW = (
        15, 20, 21, 22, 23, 24, 25, 26, 27, 28, 29)
    own, own_z = at(r, hs), at(z, zs)

    @pl.when(r == c)
    def _():
        for i in rows:
            copy(p.at[:, at(i, hs)], pc.at[:, at(i, hs)], PC_S, "row", i).start()
        pc[:, own] = p[:, own]

    @pl.when(r == 0)
    def _():
        for i in rows:
            copy(p.at[k, at(i, hs)], cm.at[P0, k, at(i, hs)], P0_S, "row", i).start()
            copy(a.at[:, at(i, hs)], a0c.at[:, at(i, hs)], A0_S, "row", i).start()
        cm[P0, k, own] = p[k, own]
        a0c[:, own] = a[:, own]

    @pl.when(c == 0)
    def _():
        for j in cols:
            kk, zz = lax.rem(j, 2), lax.div(j, 2)
            copy(a.at[kk, at(zz, zs)], fr.at[kk, at(zz, zs)], FR_S, "col", j).start()
        fr[k, own_z] = a[k, own_z]

    panel = p[...].reshape(512, 512)
    half = pl.ds(pl.multiple_of(k * 256, 256), 256)
    gp[...] = dotg(jnp.concatenate([p[0, :, half], p[1, :, half]], axis=0), panel, 0, 0)
    for i in rows:
        copy(gp.at[at(i, hs)], grs.at[r], G_RS, "row", i).start()
    grs[r] = gp[own]
    bp[...] = dot3(panel, a[...].reshape(512, 512), 0, 0).reshape(2, 256, 512)
    for i in rows:
        copy(bp.at[:, at(i, hs)], brs.at[r], B_RS, "row", i).start()
    brs[r] = bp[:, own]

    @pl.when(r != 0)
    def _():
        wait(cm.at[P0, k, own], P0_S)
        wait(a0c.at[:, own], A0_S)

    for i in rows:
        copy(cm.at[P0, k, own], cm.at[P0, k, own], CM_AG + P0, "row", i).start()

    wait(grs.at[pl.ds(0, n - 1)], G_RS)
    cm[G, k, own] = jnp.sum(grs[...], axis=0)
    for i in rows:
        copy(cm.at[G, k, own], cm.at[G, k, own], CM_AG + G, "row", i).start()

    @pl.when(r != c)
    def _():
        wait(pc.at[:, own], PC_S)

    for i in rows:
        copy(pc.at[:, own], pc.at[:, own], PC_AG, "row", i).start()

    @pl.when(c != 0)
    def _():
        wait(fr.at[k, own_z], FR_S)

    for j in cores:
        copy(fr.at[k, own_z], fr.at[k, own_z], FR_AG, "col", j).start()

    wait(brs.at[pl.ds(0, n - 1)], B_RS)
    bct[:, own] = jnp.sum(brs[...], axis=0)
    for i in rows:
        copy(bct.at[:, own], bct.at[:, own], BC_AG, "row", i).start()

    @pl.when(c == 0)
    def _():
        for j in cols:
            kk = lax.rem(j, 2)
            copy(bct.at[kk, own], cm.at[B0, kk, own], B0_S, "col", j).start()
            copy(a0c.at[kk, own], cm.at[F0, kk, own], F0_S, "col", j).start()
        cm[B0, k, own] = bct[k, own]
        cm[F0, k, own] = a0c[k, own]

    for i in rows:
        copy(a0c.at[:, own], a0c.at[:, own], A0_AG, "row", i).start()

    def gathered(item):
        wait(cm.at[item, k, pl.ds(0, 256 - hs)], CM_AG + item)
        copy(cm.at[item, k], cm.at[item, k], CM_SW + item, "col", partner).start()

    gathered(G)
    gathered(P0)

    wait(pc.at[:, pl.ds(0, 256 - hs)], PC_AG)
    pcw = split(pc[...].reshape(512, 512))
    rp[...] = dot3(bct[:, own].reshape(2 * hs, 512), pcw, 1, 0).reshape(4, ps, 512)
    where = [(h + 2 * q * max(1, zc // 4), 2 * h + q, h, q) for h in range(2) for q in range(2)]
    for dst, piece, h, q in where:
        @pl.when(c != dst)
        def _():
            copy(rp.at[piece], rrs.at[c], R_RS, "col", dst).start()

        @pl.when(c == dst)
        def _():
            rrs[c] = rp[piece]

    bq[...] = dot3(a[...].reshape(512, 512), pcw, 1, 0).reshape(2, 256, 512)
    copy(bq.at[1 - k], bsw, BQ_SW, "col", partner).start()

    @pl.when(c != 0)
    def _():
        wait(cm.at[B0, k, own], B0_S)
        wait(cm.at[F0, k, own], F0_S)

    for i in rows:
        copy(cm.at[B0, k, own], cm.at[B0, k, own], CM_AG + B0, "row", i).start()
    for i in rows:
        copy(cm.at[F0, k, own], cm.at[F0, k, own], CM_AG + F0, "row", i).start()

    for dst, piece, h, q in where:
        @pl.when(c == dst)
        def _():
            wait(rrs.at[pl.ds(0, n - 1)], R_RS)
            sl = pl.ds(pl.multiple_of(r * hs + q * ps, ps), ps)
            cm[R, h, sl] = jnp.sum(rrs[...], axis=0)
            for j in cores:
                copy(cm.at[R, h, sl], cm.at[R, h, sl], R_B, "col", j).start()

    wait(bsw, BQ_SW)
    bsum[...] = bq[k] + bsw[...]
    for j in cores:
        copy(bsum.at[at(lax.div(j, 2), zs)], bz.at[z], B_Z, "col", j).start()
    bz[z] = bsum[own_z]

    reducer = functools.reduce(jnp.logical_or, [c == dst for dst, *_ in where])

    @pl.when(reducer)
    def _():
        wait(rrs.at[0], R_B)

    @pl.when(jnp.logical_not(reducer))
    def _():
        wait(rrs.at[pl.ds(0, 2)], R_B)

    for i in rows:
        copy(cm.at[R, k, own], cm.at[R, k, own], CM_AG + R, "row", i).start()

    wait(fr.at[k, pl.ds(0, 256 - zs)], FR_AG)
    copy(fr.at[k], fr.at[k], FR_SW, "col", partner).start()

    wait(bz.at[pl.ds(0, zc - 1)], B_Z)
    br[k, own_z] = jnp.sum(bz[...], axis=0)
    for j in cores:
        copy(br.at[k, own_z], br.at[k, own_z], BR_AG, "col", j).start()

    gathered(B0)
    gathered(F0)
    gathered(R)
    wait(br.at[k, pl.ds(0, 256 - zs)], BR_AG)
    copy(br.at[k], br.at[k], BR_SW, "col", partner).start()

    wait(bct.at[:, pl.ds(0, 256 - hs)], BC_AG)
    wait(a0c.at[:, pl.ds(0, 256 - hs)], A0_AG)
    for item in range(5):
        wait(cm.at[item, 1 - k], CM_SW + item)
    wait(fr.at[1 - k], FR_SW)
    wait(br.at[1 - k], BR_SW)

    big, small = pc.at[:, pl.ds(0, 256 - hs)], bsw.at[pl.ds(0, 256 - hs)]
    zbig = bsw.at[pl.ds(0, 256 - zs)]

    @pl.when(r == c)
    def _():
        wait(big, PC_S, send)

    @pl.when(r == 0)
    def _():
        wait(small, P0_S, send)
        wait(big, A0_S, send)

    @pl.when(c == 0)
    def _():
        wait(fr.at[:, pl.ds(0, 256 - zs // 2)], FR_S, send)
        wait(small, B0_S, send)
        wait(small, F0_S, send)

    for s in (B_RS, PC_AG, A0_AG, BC_AG):
        wait(big, s, send)
    for s in (G_RS, CM_AG, CM_AG + 1, CM_AG + 2, CM_AG + 3, CM_AG + 4):
        wait(small, s, send)
    for s in (CM_SW, CM_SW + 1, CM_SW + 2, CM_SW + 3, CM_SW + 4, BQ_SW, BR_SW, FR_SW):
        wait(bsw, s, send)
    for s in (B_Z, BR_AG, FR_AG):
        wait(zbig, s, send)

    @pl.when(reducer)
    def _():
        wait(rrs.at[pl.ds(0, 3)], R_RS, send)
        wait(rrs.at[pl.ds(0, zc - 1)], R_B, send)

    @pl.when(jnp.logical_not(reducer))
    def _():
        wait(rrs.at[pl.ds(0, 4)], R_RS, send)


def final_kernel(a, p, cm, pc, bct, a0c, br, fr, li, out, x, e, s, yt):
    r, c = lax.axis_index("row"), lax.axis_index("col")

    def whole(ref):
        return ref[...].reshape(512, 512)

    eye = (
        lax.broadcasted_iota(jnp.int32, (512, 512), 0)
        == lax.broadcasted_iota(jnp.int32, (512, 512), 1)
    ).astype(F32)
    lis = split(li[...])
    start = 0.9
    m = eye + dot3(lis, cm[P0].reshape(512, 512), 1, 1)
    e[...] = eye - start * m
    x[...] = start * (eye + e[...])

    def size(value):
        return jnp.sum(value * value)

    def more(state):
        step, now = state
        return jnp.logical_and(step < 48, now > 1e-3)

    def square(state):
        step, _ = state
        es = split(e[...])
        ee = dot3(es, es, 1, 0)
        e[...] = ee
        x[...] += dot3(x[...], ee, 1, 0)
        return step + 1, size(ee)

    lax.while_loop(more, square, (jnp.int32(0), jnp.float32(1.0)))
    xs = split(x[...])
    rest = eye - dot3(m, xs, 1, 0)
    inv = x[...] + dot3(xs, rest, 1, 0)
    nis = split(dot3(inv, lis, 1, 0))

    kt = dot3(lis, cm[B0].reshape(512, 512), 1, 0)
    s[...] = (
        dot3(lis, dot3(cm[R].reshape(512, 512), lis, 1, 1), 1, 0)
        + kt + kt.T + cm[F0].reshape(512, 512)
    )
    yt[...] = jnp.where(c == 0, eye, dot3(nis, whole(pc), 1, 1))
    yts = split(yt[...])
    zt = dot3(lis, whole(bct), 1, 0) + whole(a0c) - dot3(s[...], yts, 1, 0)
    y = jnp.where(r == 0, eye, dot3(whole(p), nis, 1, 1))
    u = dot3(whole(br), lis, 1, 1) + whole(fr)
    out[...] = whole(a) - dot3(y, zt, 1, 0) - dot3(u, yts, 1, 0)


def solution(mesh):
    n = mesh.shape["row"]
    hs, zc = 256 // n, n // 2
    zs, ps = 256 // zc, 128 // n
    vm = pl.BlockSpec(memory_space=pltpu.VMEM)
    sq = jax.ShapeDtypeStruct((512, 512), F32)
    two = jax.ShapeDtypeStruct((2, 256, 512), F32)

    def step(trailing, panel):
        a, p = trailing.reshape(2, 256, 512), panel.reshape(2, 256, 512)
        cm, pc, bct, a0c, br, fr = pl.pallas_call(
            functools.partial(comm_kernel, n),
            out_shape=[jax.ShapeDtypeStruct((5, 2, 256, 512), F32)] + [two] * 5,
            in_specs=[vm] * 2,
            out_specs=[vm] * 6,
            scratch_shapes=[
                pltpu.VMEM((256, 512), F32),
                pltpu.VMEM((2, 256, 512), F32),
                pltpu.VMEM((n, hs, 512), F32),
                pltpu.VMEM((n, 2, hs, 512), F32),
                pltpu.VMEM((4, ps, 512), F32),
                pltpu.VMEM((n, ps, 512), F32),
                pltpu.VMEM((2, 256, 512), F32),
                pltpu.VMEM((256, 512), F32),
                pltpu.VMEM((256, 512), F32),
                pltpu.VMEM((zc, zs, 512), F32),
                pltpu.SemaphoreType.DMA((32,)),
                pltpu.SemaphoreType.DMA((32,)),
            ],
            compiler_params=pltpu.CompilerParams(collective_id=0, has_side_effects=True),
            name="exchange",
        )(a, p)
        nu, li = pl.pallas_call(
            factor_kernel,
            out_shape=[sq, sq],
            in_specs=[vm],
            out_specs=[vm] * 2,
            scratch_shapes=[pltpu.VMEM((512, 512), F32)] * 2,
            name="factor",
        )(cm[G])
        out = pl.pallas_call(
            final_kernel,
            out_shape=sq,
            in_specs=[vm] * 9,
            out_specs=vm,
            scratch_shapes=[pltpu.VMEM((512, 512), F32)] * 4,
            name="update",
        )(a, p, cm, pc, bct, a0c, br, fr, li)
        return out, nu

    return jax.shard_map(
        step, mesh=mesh, in_specs=(P("row", "col"), P("row", None)),
        out_specs=(P("row", "col"), P()), check_vma=False,
    )
```

time: 805 us -> 171 us (0.21)
  the two profiles are of different devices: /device:TPU:32 before, /device:TPU:93 now
where the time goes in v1:
time: 171 us
  Pallas kernels  168 us (98%)
  local copies, waits for them, and re-layouts  2.26 us (1%)
    pallas_call x1, Pallas kernels, step(): pl.pallas_call(functools.partial(comm_kernel, n), out_shape=[jax.ShapeDty...  120 us
    pallas_call x1, Pallas kernels, step(): pl.pallas_call(final_kernel, out_shape=sq, in_specs=[vm] * 9, out_specs=v...  24 us
    pallas_call x1, Pallas kernels, step(): pl.pallas_call(factor_kernel, out_shape=[sq, sq], in_specs=[vm], out_spec...  23.9 us

profile of v1, /device:TPU:93, one launch (start us, length us, event | category | flops | bytes accessed | tf_op | source)
XLA Modules:
  0.0 171.3 jit_solution(11868490127123407856)
XLA Ops:
  0.6 120.4 %exchange.1 = (f32[5,2,256,512]{3,2,1,0:T(8,128)}, f32[2,256,512]{2,1,0:T(8,128)}, f32[2,256,512]{2,1,0:T(8,128)}, f32[2,256,512]{2,1,0:T(8,128)}, f32[2,256,512]{2,1,0:T(8,128)}, /*index=5*/f32[2,256,512]{2,1,0:T(8,128)}) custom-call(f32[2,256,512]{2,1,0:T(8,128)} %bitcast.4, f32[2,256,512]{2,1,0:T(8,128)} %bitcast.6), custom_call_target="tpu_custom_call" | custom-call | tf_op jit(solution)/shard_map/exchange/pallas_call | solution.py:397
  121.1 2.3 %slice_bitcast_fusion.g = f32[2,256,512]{2,1,0:T(8,128)} fusion(f32[5,2,256,512]{3,2,1,0:T(8,128)} %get-tuple-element.10.cm), kind=kLoop, calls=%fused_computation | loop fusion | bytes 2097152 | tf_op jit(solution)/shard_map/squeeze | solution.py:426
  123.3 23.9 %factor.1 = (f32[512,512]{1,0:T(8,128)}, f32[512,512]{1,0:T(8,128)}) custom-call(f32[2,256,512]{2,1,0:T(8,128)} %slice_bitcast_fusion.g), custom_call_target="tpu_custom_call" | custom-call | tf_op jit(solution)/shard_map/factor/pallas_call | solution.py:419
  147.3 24.0 %update.1 = f32[512,512]{1,0:T(8,128)} custom-call(f32[2,256,512]{2,1,0:T(8,128)} %bitcast.5, f32[2,256,512]{2,1,0:T(8,128)} %bitcast.7, f32[5,2,256,512]{3,2,1,0:T(8,128)} %get-tuple-element.10.cm, f32[2,256,512]{2,1,0:T(8,128)} %get-tuple-element.11.pc, f32[2,256,512]{2,1,0:T(8,128)} %get-tuple-element.12.bct, f32[2,256,512]{2,1,0:T(8,128)} %get-tuple-element.13.a0c, ...), custom_call_target="tpu_custom_call" | custom-call | tf_op jit(solution)/shard_map/update/pallas_call | solution.py:427

commit v2 on v0

v2 whole, which is shorter than its diff:
```python
import functools
import jax
import jax.numpy as jnp
from jax import lax
from jax.experimental import pallas as pl
from jax.experimental.pallas import tpu as pltpu
from jax.sharding import PartitionSpec as P

HI = lax.Precision.HIGHEST
F32 = jnp.float32
BF16 = jnp.bfloat16
MESH = pl.DeviceIdType.MESH
G, P0, B0, F0, R = range(5)


def dotg(a, b, ca, cb):
    return lax.dot_general(
        a, b, (((ca,), (cb,)), ((), ())), precision=HI, preferred_element_type=F32
    )


def split(x):
    high = x.astype(BF16)
    return high, (x - high.astype(F32)).astype(BF16)


def dot3(a, b, ca, cb):
    ah, al = a if isinstance(a, tuple) else split(a)
    bh, bl = b if isinstance(b, tuple) else split(b)
    dims = (((ca,), (cb,)), ((), ()))
    d = functools.partial(lax.dot_general, dimension_numbers=dims, preferred_element_type=F32)
    return d(ah, bh) + (d(ah, bl) + d(al, bh))


def bc(x):
    return jnp.broadcast_to(x, (8, 128))


def leaf(d, pause):
    sub = lax.broadcasted_iota(jnp.int32, (8, 128), 0)
    lane = lax.broadcasted_iota(jnp.int32, (8, 128), 1)
    d = list(d)
    inv = [(lane == sub + 8 * q).astype(F32) for q in range(16)]
    upper, lower_inv = [], []
    for q in range(16):
        cb = [bc(d[q][:, 8 * q + j : 8 * q + j + 1]) for j in range(8)]
        mul = [[bc(d[p][:, 8 * q + j : 8 * q + j + 1]) for j in range(8)] for p in range(q + 1, 16)]
        zd, zi = d[q], inv[q]
        ud = jnp.zeros((8, 128), F32)
        ui = ud
        for j in range(8):
            pivot = bc(cb[j][j : j + 1, :])
            r = 1.0 / pivot
            rs = lax.rsqrt(pivot)
            rd, ri = bc(zd[j : j + 1, :]), bc(zi[j : j + 1, :])
            mine = sub == j
            ud, ui = jnp.where(mine, rd * rs, ud), jnp.where(mine, ri * rs, ui)
            pd, pi = rd * r, ri * r
            zd = jnp.where(mine, pd, zd - cb[j] * pd)
            zi = jnp.where(mine, pi, zi - cb[j] * pi)
            for k in range(j + 1, 8):
                t = bc(cb[k][j : j + 1, :]) * r
                cb[k] = jnp.where(mine, t, cb[k] - cb[j] * t)
        upper.append(jnp.where(lane >= sub + 8 * q, ud, 0.0))
        lower_inv.append(ui)
        zds = [bc(zd[j : j + 1, :]) for j in range(8)]
        zis = [bc(zi[j : j + 1, :]) for j in range(8)]
        for p in range(q + 1, 16):
            m = mul[p - q - 1]
            x, y = d[p], inv[p]
            for j in range(8):
                x, y = x - m[j] * zds[j], y - m[j] * zis[j]
            d[p], inv[p] = x, y
        if q in (3, 7, 11):
            pause()
    return upper, lower_inv


def factor_block(b, w, u, li, pause):
    s, e = 128 * b, 128 * b + 128
    upper, lower_inv = leaf([w[s + 8 * q : s + 8 * q + 8, s:e] for q in range(16)], pause)
    for q in range(16):
        u[s + 8 * q : s + 8 * q + 8, s:e] = upper[q]
        li[s + 8 * q : s + 8 * q + 8, s:e] = lower_inv[q]
    lb = li[s:e, s:e]
    if b < 3:
        u[s:e, e:] = dotg(lb, w[s:e, e:], 1, 0)
    if b > 0:
        li[s:e, :s] = dotg(lb, li[s:e, :s], 1, 0)
    if b < 3:
        ut = u[s:e, e:]
        w[e:, e:] -= dotg(ut, ut, 0, 0)
        li[e:, :e] -= dotg(ut, li[s:e, :e], 0, 0)


NAMES = ["pc_s", "p0_s", "a0_s", "fr_s", "g_rs", "b0_s", "f0_s", "r_rs"]
NAMES += ["r_b", "bq_w", "bz", "br_g", "br_w", "fr_g", "fr_w"]
NAMES += [(item, step) for item in ("pc", "bc", "a0", "rs") for step in range(4)]
NAMES += [(item, step) for item in range(5) for step in range(5)]
SEM = {name: i for i, name in enumerate(NAMES)}


def main_kernel(
    nx, a, p, nu, li, m, s, ut, u, pc,
    cm, bct, a0c, br, fr, gp, bp, grs, rb1, rb2, rb3, rb4, rp, rrs, bq, bsw, bsum, bz, w, up, send, recv,
):
    n = nx * nx
    zc, part = n // 2, nx - 1
    r, c = lax.axis_index("row"), lax.axis_index("col")
    y, x = lax.div(r, nx), lax.rem(r, nx)
    z, k = lax.div(c, 2), lax.rem(c, 2)
    partner = c + 1 - 2 * k

    def copy(src, dst, name, axis, index):
        pltpu.make_async_remote_copy(
            src_ref=src, dst_ref=dst, send_sem=send.at[SEM[name]], recv_sem=recv.at[SEM[name]],
            device_id={axis: index}, device_id_type=MESH,
        ).start()

    def wait(ref, name, sems=recv):
        pltpu.make_async_copy(ref, ref, sems.at[SEM[name]]).wait()

    rows = [lax.rem(r + j, n) for j in range(1, n)]
    cols = [lax.rem(c + j, n) for j in range(1, n)]
    cores = [lax.rem(c + 2 * j, n) for j in range(1, zc)]
    def near(v, way):
        one = v + 1 - 2 * lax.rem(v, 2)
        two = lax.rem(v - 1 + 2 * lax.rem(v, 2) + nx, nx)
        return jnp.where(way == 0, one, two)

    def line(zz):
        return lax.div(2 * zz, nx), pl.ds(lax.rem(2 * zz, nx), 2)

    own_line = line(z)

    barrier = pltpu.get_barrier_semaphore()
    for i in rows:
        pl.semaphore_signal(barrier, inc=1, device_id={"row": i}, device_id_type=MESH)
    for i in cols:
        pl.semaphore_signal(barrier, inc=1, device_id={"col": i}, device_id_type=MESH)
    pl.semaphore_wait(barrier, 2 * n - 2)

    every = slice(None)
    steps = 4 if nx == 4 else 2

    def plan(first, way):
        ya, xa = near(y, way), near(x, way)
        yb, xb = near(y, 1 - way), near(x, 1 - way)
        along_x, along_y = [([(y, x)], y * nx + xa)], [([(y, x)], ya * nx + x)]
        if nx == 4:
            along_x.append(([(y, x), (y, xa)], y * nx + xb))
            along_y.append(([(y, x), (ya, x)], yb * nx + x))
        if first == 0:
            along_x.append(([(y, every)], ya * nx + x))
            if nx == 4:
                along_x.append(([(y, every), (ya, every)], yb * nx + x))
            return along_x
        along_y.append(([(every, x)], y * nx + xa))
        if nx == 4:
            along_y.append(([(every, x), (every, xa)], y * nx + xb))
        return along_y

    full_parts = [((kk, h), plan(h, kk)) for kk in range(2) for h in range(2)]
    half_parts = [(h, plan(h, k)) for h in range(2)]

    def full_got(ref, step):
        return (ref.at[:, 0, 0], ref.at[:, 0, pl.ds(0, 2)], ref.at[:, 0], ref.at[:, pl.ds(0, 2)])[
            step if nx == 4 else 2 * step
        ]

    def half_got(it, step):
        ref = cm.at[it, k]
        return (ref.at[0, 0], ref.at[0, pl.ds(0, 2)], ref.at[0], ref.at[pl.ds(0, 2)])[
            step if nx == 4 else 2 * step
        ]

    def full(ref, item, step):
        if step > steps:
            return
        if step > 0:
            wait(full_got(ref, step - 1), (item, step - 1))
        if step == steps:
            return
        for (kk, h), moves in full_parts:
            pieces, target = moves[step]
            for v, u_ in pieces:
                copy(ref.at[kk, v, u_, h], ref.at[kk, v, u_, h], (item, step), "row", target)

    def half(it, step):
        if step > steps:
            return
        if step > 0:
            wait(half_got(it, step - 1), (it, step - 1))
        if step == steps:
            copy(cm.at[it, k], cm.at[it, k], (it, 4), "col", partner)
            return
        for h, moves in half_parts:
            pieces, target = moves[step]
            for v, u_ in pieces:
                copy(cm.at[it, k, v, u_, h], cm.at[it, k, v, u_, h], (it, step), "row", target)

    def half_end(it):
        wait(cm.at[it, 1 - k], (it, 4))

    halves = (rb1, rb2, rb3, rb4)

    def reduce_step(step):
        if nx == 2 and step in (0, 2):
            return
        for kk in range(2):
            for h in range(2):
                at = 2 * kk + h
                on_y = (h == 0) == (step < 2)
                v = y if on_y else x
                near_a, near_b = near(v, kk), near(v, 1 - kk)
                goal = near_b if step % 2 == 0 else near_a
                target = goal * nx + x if on_y else y * nx + goal
                taken = [goal, near(goal, kk)] if step % 2 == 0 else [goal]
                for j, index in enumerate(taken):
                    other = every if step < 2 else (x if on_y else y)
                    src = bp.at[kk, index, other, h] if on_y else bp.at[kk, other, index, h]
                    dst = halves[step].at[at, j] if step % 2 == 0 else halves[step].at[at]
                    copy(src, dst, ("rs", step), "row", target)

    def reduce_add(step):
        if nx == 2 and step in (0, 2):
            return
        wait(halves[step], ("rs", step))
        for kk in range(2):
            for h in range(2):
                at = 2 * kk + h
                on_y = (h == 0) == (step < 2)
                v = y if on_y else x
                kept = [v, near(v, kk)] if step % 2 == 0 else [v]
                for j, index in enumerate(kept):
                    other = every if step < 2 else (x if on_y else y)
                    got = halves[step][at, j] if step % 2 == 0 else halves[step][at]
                    where_ = (kk, index, other, h) if on_y else (kk, other, index, h)
                    bp[where_] += got

    def whole(ref):
        return ref[...].reshape(512, 512)

    panel = whole(p)
    mine = pl.ds(pl.multiple_of(k * 256, 256), 256)
    w[...] = panel
    gp[...] = dotg(w[:, mine], panel, 0, 0).reshape(gp.shape)
    for i in rows:
        copy(gp.at[lax.div(i, nx), lax.rem(i, nx)], grs.at[r], "g_rs", "row", i)
    grs[r] = gp[y, x]

    @pl.when(r == c)
    def _():
        for i in rows:
            v, h = lax.div(i, nx), lax.rem(i, nx)
            copy(p.at[:, v, h], pc.at[:, v, h], "pc_s", "row", i)
        pc[:, y, x] = p[:, y, x]

    @pl.when(c == 0)
    def _():
        for j in cols:
            kk, (v, h) = lax.rem(j, 2), line(lax.div(j, 2))
            copy(a.at[kk, v, h], fr.at[kk, v, h], "fr_s", "col", j)
        fr[(k, *own_line)] = a[(k, *own_line)]

    bp[...] = dot3(panel, whole(a), 0, 0).reshape(bp.shape)
    reduce_step(0 if nx == 4 else 1)

    wait(grs.at[pl.ds(0, n - 1)], "g_rs")
    cm[G, k, y, x] = jnp.sum(grs[...], axis=0)
    where = [(h + 2 * q * max(1, zc // 4), h, q) for h in range(2) for q in range(2)]
    reducer = functools.reduce(jnp.logical_or, [c == dst for dst, *_ in where])

    def b_step(step):
        def run():
            if nx == 2 and step == 2:
                reduce_add(1)
                reduce_step(3)
            elif nx == 4:
                reduce_add(step - 1)
                reduce_step(step)
        return run

    def b_done():
        reduce_add(3)
        bct[:, y, x] = bp[:, y, x]
        full(bct, "bc", 0)

        @pl.when(c == 0)
        def _():
            for j in cols:
                kk = lax.rem(j, 2)
                copy(bct.at[kk, y, x], cm.at[B0, kk, y, x], "b0_s", "col", j)
            cm[B0, k, y, x] = bct[k, y, x]

    def pc_start():
        @pl.when(r != c)
        def _():
            wait(pc.at[:, y, x], "pc_s")

        full(pc, "pc", 0)

    def a0_start():
        @pl.when(r != 0)
        def _():
            wait(a0c.at[:, y, x], "a0_s")

        full(a0c, "a0", 0)

        @pl.when(c == 0)
        def _():
            for j in cols:
                kk = lax.rem(j, 2)
                copy(a0c.at[kk, y, x], cm.at[F0, kk, y, x], "f0_s", "col", j)
            cm[F0, k, y, x] = a0c[k, y, x]

    def p0_start():
        @pl.when(r != 0)
        def _():
            wait(cm.at[P0, k, y, x], "p0_s")

        half(P0, 0)

    def fr_start():
        @pl.when(c != 0)
        def _():
            wait(fr.at[(k, *own_line)], "fr_s")

        for j in cores:
            copy(fr.at[(k, *own_line)], fr.at[(k, *own_line)], "fr_g", "col", j)

    def fr_swap():
        wait(bz.at[pl.ds(0, zc - 1)], "fr_g")
        copy(fr.at[k], fr.at[k], "fr_w", "col", partner)

    def bq_start():
        full(pc, "pc", steps)
        bq[...] = dot3(whole(a), whole(pc), 1, 0).reshape(bq.shape)
        copy(bq.at[1 - k], bsw, "bq_w", "col", partner)

    def rp_start():
        rp[...] = dot3(bct[:, y, x].reshape(512 // n, 512), whole(pc), 1, 0).reshape(rp.shape)
        for dst, h, q in where:
            @pl.when(c != dst)
            def _():
                copy(rp.at[h, q], rrs.at[c], "r_rs", "col", dst)

            @pl.when(c == dst)
            def _():
                rrs[c] = rp[h, q]

    def br_reduce():
        wait(bsw, "bq_w")
        bsum[...] = bq[k] + bsw[...]
        for j in cores:
            copy(bsum.at[line(lax.div(j, 2))], bz.at[z], "bz", "col", j)
        bz[z] = bsum[own_line]

    def br_start():
        wait(bz.at[pl.ds(0, zc - 1)], "bz")
        br[(k, *own_line)] = jnp.sum(bz[...], axis=0)
        for j in cores:
            copy(br.at[(k, *own_line)], br.at[(k, *own_line)], "br_g", "col", j)

    def br_swap():
        wait(bz.at[pl.ds(0, zc - 1)], "br_g")
        copy(br.at[k], br.at[k], "br_w", "col", partner)

    def r_reduce():
        for dst, h, q in where:
            @pl.when(c == dst)
            def _():
                wait(rrs.at[pl.ds(0, n - 1)], "r_rs")
                cm[R, h, y, x, q] = jnp.sum(rrs[...], axis=0)
                for j in cores:
                    copy(cm.at[R, h, y, x, q], cm.at[R, h, y, x, q], "r_b", "col", j)

    def r_start():
        @pl.when(reducer)
        def _():
            wait(rrs.at[0], "r_b")

        @pl.when(jnp.logical_not(reducer))
        def _():
            wait(rrs.at[pl.ds(0, 2)], "r_b")

        half(R, 0)

    def b0_start():
        @pl.when(c != 0)
        def _():
            wait(cm.at[B0, k, y, x], "b0_s")

        half(B0, 0)

    def f0_start():
        @pl.when(c != 0)
        def _():
            wait(cm.at[F0, k, y, x], "f0_s")

        half(F0, 0)

    def f(ref, item, step):
        return lambda: full(ref, item, step) if step < steps else None

    def g(it, step):
        return lambda: half(it, step)

    def spread_p0():
        @pl.when(r == 0)
        def _():
            for i in rows:
                v, h = lax.div(i, nx), lax.rem(i, nx)
                copy(p.at[k, v, h], cm.at[P0, k, v, h], "p0_s", "row", i)
            cm[P0, k, y, x] = p[k, y, x]

    def spread_a0(part):
        def run():
            @pl.when(r == 0)
            def _():
                for i in rows[part::5]:
                    v, h = lax.div(i, nx), lax.rem(i, nx)
                    copy(a.at[:, v, h], a0c.at[:, v, h], "a0_s", "row", i)
                if part == 0:
                    a0c[:, y, x] = a[:, y, x]
        return run

    before = [
        g(G, 0), pc_start, spread_a0(0), g(G, 1), b_step(1), fr_start, spread_a0(1),
        g(G, 2), f(pc, "pc", 1), b_step(2), spread_a0(2), g(G, 3), f(pc, "pc", 2), b_step(3),
        spread_a0(3), g(G, 4), f(pc, "pc", 3), b_done, spread_a0(4), spread_p0,
    ]
    for action in before:
        action()

    hooks = [
        [],
        [bq_start],
        [rp_start, f(bct, "bc", 1), a0_start],
        [f(bct, "bc", 2), p0_start, b0_start],
        [r_reduce, br_reduce, f(a0c, "a0", 1)],
        [f(bct, "bc", 3), g(P0, 1), g(B0, 1)],
        [r_start, f(a0c, "a0", 2), f0_start],
        [g(P0, 2), g(B0, 2), g(R, 1)],
        [f(a0c, "a0", 3), g(F0, 1)],
        [g(P0, 3), g(R, 2), g(B0, 3)],
        [g(F0, 2)],
        [g(P0, 4), g(R, 3), g(B0, 4), br_start],
        [g(F0, 3), fr_swap],
        [g(R, 4)],
        [g(F0, 4)],
        [],
    ]

    left = list(hooks)

    def pause():
        for action in left.pop(0):
            action()

    half_end(G)
    w[...] = cm[G].reshape(512, 512)
    up[...] = jnp.zeros((512, 512), F32)
    li[...] = jnp.zeros((512, 512), F32)
    for b in range(4):
        factor_block(b, w, up, li, pause)
        pause()
    nu[...] = -up[...]

    eye = (
        lax.broadcasted_iota(jnp.int32, (512, 512), 0)
        == lax.broadcasted_iota(jnp.int32, (512, 512), 1)
    ).astype(F32)
    lis = split(li[...])
    half_end(P0)
    m[...] = eye + dot3(lis, cm[P0].reshape(512, 512), 1, 1)
    full(a0c, "a0", steps)
    full(bct, "bc", steps)
    ut[...] = dot3(lis, whole(bct), 1, 0) + whole(a0c)
    br_swap()
    half_end(B0)
    half_end(F0)
    s[...] = dot3(lis, cm[B0].reshape(512, 512), 1, 0)
    s[...] += s[...].T + cm[F0].reshape(512, 512)
    half_end(R)
    s[...] += dot3(lis, dot3(cm[R].reshape(512, 512), lis, 1, 1), 1, 0)
    wait(br.at[1 - k], "br_w")
    wait(fr.at[1 - k], "fr_w")
    u[...] = dot3(whole(br), lis, 1, 1) + whole(fr)

    scattered = grs.at[pl.ds(0, n - 1)]

    slices = cm.at[:, :, 0, pl.ds(0, 3)] if nx == 4 else cm.at[pl.ds(0, 3), :, 0, 0]

    def wait_slices(name, sems):
        wait(slices, name, sems)

    @pl.when(r == c)
    def _():
        wait_slices( "pc_s", send)

    @pl.when(r == 0)
    def _():
        wait(scattered, "p0_s", send)
        wait_slices( "a0_s", send)

    @pl.when(c == 0)
    def _():
        wait_slices( "fr_s", send)
        wait(scattered, "b0_s", send)
        wait(scattered, "f0_s", send)

    wait(scattered, "g_rs", send)
    for step in range(steps):
        for item in ("pc", "bc", "a0"):
            wait(full_got(pc, step), (item, step), send)
        for it in range(5):
            wait(half_got(it, step), (it, step), send)
    for step in range(4):
        if nx == 4 or step in (1, 3):
            wait(halves[step], ("rs", step), send)
    for name in ("bq_w", "br_w", "fr_w", *((it, 4) for it in range(5))):
        wait(cm.at[0, 0], name, send)
    for name in ("bz", "br_g", "fr_g"):
        wait(bz.at[pl.ds(0, zc - 1)], name, send)

    @pl.when(reducer)
    def _():
        wait(rrs.at[pl.ds(0, 3)], "r_rs", send)
        wait(rrs.at[pl.ds(0, zc - 1)], "r_b", send)

    @pl.when(jnp.logical_not(reducer))
    def _():
        wait(rrs.at[pl.ds(0, 4)], "r_rs", send)


def final_kernel(a, p, li, m, s, ut, u, pc, out, xx, e):
    r, c = lax.axis_index("row"), lax.axis_index("col")
    eye = (
        lax.broadcasted_iota(jnp.int32, (512, 512), 0)
        == lax.broadcasted_iota(jnp.int32, (512, 512), 1)
    ).astype(F32)
    start = 0.9
    e[...] = eye - start * m[...]
    xx[...] = start * (eye + e[...])

    def more(state):
        step, now = state
        return jnp.logical_and(step < 48, now > 1e-3)

    def square(state):
        step, _ = state
        es = split(e[...])
        ee = dot3(es, es, 1, 0)
        e[...] = ee
        xx[...] += dot3(xx[...], ee, 1, 0)
        return step + 1, jnp.sum(ee * ee)

    lax.while_loop(more, square, (jnp.int32(0), jnp.float32(1.0)))
    xs = split(xx[...])
    rest = eye - dot3(m[...], xs, 1, 0)
    inv = xx[...] + dot3(xs, rest, 1, 0)
    nis = split(dot3(inv, li[...], 1, 0))
    yts = split(jnp.where(c == 0, eye, dot3(nis, pc[...], 1, 1)))
    zt = ut[...] - dot3(s[...], yts, 1, 0)
    y = jnp.where(r == 0, eye, dot3(p[...], nis, 1, 1))
    out[...] = a[...] - dot3(y, zt, 1, 0) - dot3(u[...], yts, 1, 0)


def solution(mesh):
    n = mesh.shape["row"]
    nx = {4: 2, 16: 4}[n]
    zc, rr = n // 2, 128 // n
    vm = pl.BlockSpec(memory_space=pltpu.VMEM)
    sq = jax.ShapeDtypeStruct((512, 512), F32)
    shape = (2, nx, nx, 2, rr, 512)

    def scratch(*lead):
        return pltpu.VMEM((*lead, 512), F32)

    def step(trailing, panel):
        nu, li, m, s, ut, u, pc = pl.pallas_call(
            functools.partial(main_kernel, nx),
            out_shape=[sq] * 6 + [jax.ShapeDtypeStruct(shape, F32)],
            in_specs=[vm] * 2,
            out_specs=[vm] * 7,
            scratch_shapes=[
                scratch(5, *shape[:-1]),
                scratch(*shape[:-1]),
                scratch(*shape[:-1]),
                scratch(*shape[:-1]),
                scratch(*shape[:-1]),
                scratch(*shape[1:-1]),
                scratch(*shape[:-1]),
                scratch(n, 2, rr),
                scratch(4, 2, nx, rr),
                scratch(4, nx, rr),
                scratch(4, 2, rr),
                scratch(4, rr),
                scratch(2, 2, rr),
                scratch(n, rr),
                scratch(*shape[:-1]),
                scratch(*shape[1:-1]),
                scratch(*shape[1:-1]),
                scratch(zc, 2, 2, rr),
                scratch(512),
                scratch(512),
                pltpu.SemaphoreType.DMA((len(NAMES),)),
                pltpu.SemaphoreType.DMA((len(NAMES),)),
            ],
            compiler_params=pltpu.CompilerParams(collective_id=0, has_side_effects=True, vmem_limit_bytes=34 << 20),
            name="exchange_factor",
        )(trailing.reshape(shape), panel.reshape(shape))
        out = pl.pallas_call(
            final_kernel,
            out_shape=sq,
            in_specs=[vm] * 8,
            out_specs=vm,
            scratch_shapes=[pltpu.VMEM((512, 512), F32)] * 2,
            compiler_params=pltpu.CompilerParams(vmem_limit_bytes=30 << 20),
            name="update",
        )(trailing, panel, li, m, s, ut, u, pc.reshape(512, 512))
        return out, nu

    return jax.shard_map(
        step, mesh=mesh, in_specs=(P("row", "col"), P("row", None)),
        out_specs=(P("row", "col"), P()), check_vma=False,
    )
```

time: 805 us -> 111 us (0.14)
  waiting for transfers between devices: 448 us -> 0 us
  other arithmetic: 244 us -> 0 us
  Pallas kernels: 0 us -> 105 us
  matrix products: 59.1 us -> 0 us
  local copies, waits for them, and re-layouts: 25.6 us -> 3.42 us
  between operations: 20.4 us -> 0.66 us
    psum x3 -> x0, waiting for transfers between devices: 293 us -> none  [the longest x1 103 us: local(): gram_total, leading_total = lax.psum((gram_local, leading), 'row')]
    another operation x33 -> x0, other arithmetic: 237 us -> none  [the longest x15 79.7 us: local(): factor_square = jnp.linalg.cholesky(product(system, system.T))]
    pallas_call x0 -> x2, Pallas kernels: none -> 105 us  [the longest x1 90.9 us: step(): pl.pallas_call(functools.partial(main_kernel, nx), out_shape=[sq] * 6 + [...]
    all_gather x2 -> x0, waiting for transfers between devices: 81.2 us -> none  [the longest x1 42 us: spread(): lax.all_gather(own, axis, axis=0, tiled=True)[:len(lines)]]
    reduce_scatter x3 -> x0, waiting for transfers between devices: 73.5 us -> none  [the longest x2 52.3 us: own_block(): parts = lax.psum_scatter(parts, axes[k], scatter_dimension=0, tiled=True)]
    dot_general x9 -> x0, matrix products: 30.9 us -> none  [the longest x6 16 us: product(): jnp.dot(former, latter, precision=PRECISE, preferred_element_type=jnp.flo...]
    another operation x40 -> x0, matrix products: 28.2 us -> none  [the longest x14 12.6 us: local(): jax.scipy.linalg.cho_solve((factor_square, True), identity)]
    another operation x38 -> x0, local copies, waits for them, and re-layouts: 18.7 us -> none  [the longest x18 10.4 us: local(): jax.scipy.linalg.solve_triangular(lower_factor, panel_block.T, lower=True)]
  transfers between devices with their start and end apart: 8 -> 0, of which waited for: 8 -> 0; matrix products, arithmetic and copies ran while one was open for 8% -> 0% of each run, Pallas kernels for 0% -> 0%
where the time goes in v2:
time: 111 us; the launch traced here: 109 us
  Pallas kernels  105 us (95%)
  local copies, waits for them, and re-layouts  3.42 us (3%)
    pallas_call x1, Pallas kernels, step(): pl.pallas_call(functools.partial(main_kernel, nx), out_shape=[sq] * 6 + [...  90.9 us
    pallas_call x1, Pallas kernels, step(): pl.pallas_call(final_kernel, out_shape=sq, in_specs=[vm] * 8, out_specs=v...  14.1 us
    unnamed x9, local copies, waits for them, and re-layouts  3.42 us

profile of v2, /device:TPU:32, one launch (start us, length us, event | category | flops | bytes accessed | tf_op | source)
XLA Modules:
  0.0 109.1 jit_solution(8589091117710100203)
XLA Ops:
  0.6 0.0 copy-start
  0.6 1.2 %copy-done = f32[512,512]{1,0:T(8,128)S(1)} copy-done((f32[512,512]{1,0:T(8,128)S(1)}, f32[512,512]{1,0:T(8,128)}, u32[]{:S(2)}) %copy-start) | copy-done | bytes 1048600
  1.9 0.0 copy-start.2
  1.9 1.2 %copy-done.2 = f32[512,512]{1,0:T(8,128)S(1)} copy-done((f32[512,512]{1,0:T(8,128)S(1)}, f32[512,512]{1,0:T(8,128)}, u32[]{:S(2)}) %copy-start.2) | copy-done | bytes 1048600
  3.1 0.0 copy-start.1
  3.1 0.0 copy-start.3
  3.1 90.9 %exchange_factor.1 = (f32[512,512]{1,0:T(8,128)S(1)}, f32[512,512]{1,0:T(8,128)S(1)}, f32[512,512]{1,0:T(8,128)S(1)}, f32[512,512]{1,0:T(8,128)S(1)}, f32[512,51...) custom-call(f32[2,4,4,2,8,512]{5,4,3,2,1,0:T(8,128)S(1)} %bitcast.3, ...), custom_call_target="tpu_custom_call" | custom-call | tf_op jit(solution)/shard_map/exchange_factor/pallas_call | solution.py:582
  94.0 0.0 copy-done.1
  94.1 0.0 copy-done.3
  94.1 14.1 %update.1 = f32[512,512]{1,0:T(8,128)} custom-call(f32[512,512]{1,0:T(8,128)S(1)} %copy-done.1, f32[512,512]{1,0:T(8,128)S(1)} %copy-done.3, f32[512,512]{1,0:T(8,128)S(1)} %get-tuple-element.9.li, f32[512,512]{1,0:T(8,128)S(1)} %get-tuple-element.10.m, f32[512,512]{1,0:T(8,128)S(1)} %get-tuple-element.11.s, f32[512,512]{1,0:T(8,128)S(1)} %get-tuple-element.12.ut, ...), custom_call_target="tpu_custom_call" | custom-call | tf_op jit(solution)/shard_map/update/pallas_call | solution.py:614
  108.2 1.0 copy.5
Async XLA Ops:
  0.6 1.2 %copy-start = (f32[512,512]{1,0:T(8,128)S(1)}, f32[512,512]{1,0:T(8,128)}, u32[]{:S(2)}) copy-start(f32[512,512]{1,0:T(8,128)} %a.1) | copy-start | bytes 3145732
  1.9 1.2 %copy-start.2 = (f32[512,512]{1,0:T(8,128)S(1)}, f32[512,512]{1,0:T(8,128)}, u32[]{:S(2)}) copy-start(f32[512,512]{1,0:T(8,128)} %p.1) | copy-start | bytes 3145732
  3.1 91.0 %copy-start.1 = (f32[512,512]{1,0:T(8,128)S(1)}, f32[512,512]{1,0:T(8,128)}, u32[]{:S(2)}) copy-start(f32[512,512]{1,0:T(8,128)} %a.1) | copy-start | bytes 3145732
  3.1 91.0 %copy-start.3 = (f32[512,512]{1,0:T(8,128)S(1)}, f32[512,512]{1,0:T(8,128)}, u32[]{:S(2)}) copy-start(f32[512,512]{1,0:T(8,128)} %p.1) | copy-start | bytes 3145732

commit v3 on v2

--- a/solution.py
+++ b/solution.py
@@ -101,8 +101,8 @@
 
 
 def main_kernel(
-    nx, a, p, nu, li, m, s, ut, u, pc,
-    cm, bct, a0c, br, fr, gp, bp, grs, rb1, rb2, rb3, rb4, rp, rrs, bq, bsw, bsum, bz, w, up, send, recv,
+    nx, a_in, p_in, nu, li, m, s, ut, u, pc,
+    a, p, load, cm, bct, a0c, br, fr, gp, bp, grs, rb1, rb2, rb3, rb4, rp, rrs, bq, bsw, bsum, bz, w, up, send, recv,
 ):
     n = nx * nx
     zc, part = n // 2, nx - 1
@@ -133,12 +133,14 @@
 
     own_line = line(z)
 
+    loads = [pltpu.make_async_copy(p_in, p, load.at[0]), pltpu.make_async_copy(a_in, a, load.at[1])]
+    for piece in loads:
+        piece.start()
     barrier = pltpu.get_barrier_semaphore()
     for i in rows:
         pl.semaphore_signal(barrier, inc=1, device_id={"row": i}, device_id_type=MESH)
     for i in cols:
         pl.semaphore_signal(barrier, inc=1, device_id={"col": i}, device_id_type=MESH)
-    pl.semaphore_wait(barrier, 2 * n - 2)
 
     every = slice(None)
     steps = 4 if nx == 4 else 2
@@ -241,10 +243,14 @@
     def whole(ref):
         return ref[...].reshape(512, 512)
 
+    loads[0].wait()
     panel = whole(p)
     mine = pl.ds(pl.multiple_of(k * 256, 256), 256)
     w[...] = panel
     gp[...] = dotg(w[:, mine], panel, 0, 0).reshape(gp.shape)
+    loads[1].wait()
+    bp[...] = dot3(panel, whole(a), 0, 0).reshape(bp.shape)
+    pl.semaphore_wait(barrier, 2 * n - 2)
     for i in rows:
         copy(gp.at[lax.div(i, nx), lax.rem(i, nx)], grs.at[r], "g_rs", "row", i)
     grs[r] = gp[y, x]
@@ -263,7 +269,6 @@
             copy(a.at[kk, v, h], fr.at[kk, v, h], "fr_s", "col", j)
         fr[(k, *own_line)] = a[(k, *own_line)]
 
-    bp[...] = dot3(panel, whole(a), 0, 0).reshape(bp.shape)
     reduce_step(0 if nx == 4 else 1)
 
     wait(grs.at[pl.ds(0, n - 1)], "g_rs")
@@ -437,19 +442,19 @@
         [],
         [bq_start],
         [rp_start, f(bct, "bc", 1), a0_start],
-        [f(bct, "bc", 2), p0_start, b0_start],
-        [r_reduce, br_reduce, f(a0c, "a0", 1)],
+        [br_reduce, f(bct, "bc", 2), p0_start, b0_start],
+        [r_reduce, f(a0c, "a0", 1)],
         [f(bct, "bc", 3), g(P0, 1), g(B0, 1)],
-        [r_start, f(a0c, "a0", 2), f0_start],
-        [g(P0, 2), g(B0, 2), g(R, 1)],
-        [f(a0c, "a0", 3), g(F0, 1)],
-        [g(P0, 3), g(R, 2), g(B0, 3)],
-        [g(F0, 2)],
-        [g(P0, 4), g(R, 3), g(B0, 4), br_start],
+        [f(a0c, "a0", 2), f0_start],
+        [g(P0, 2), g(B0, 2)],
+        [r_start, f(a0c, "a0", 3), g(F0, 1)],
+        [g(P0, 3), g(B0, 3), br_start],
+        [g(F0, 2), g(R, 1)],
+        [g(P0, 4), g(B0, 4), g(R, 2)],
         [g(F0, 3), fr_swap],
+        [g(R, 3)],
+        [g(F0, 4)],
         [g(R, 4)],
-        [g(F0, 4)],
-        [],
     ]
 
     left = list(hooks)
@@ -534,7 +539,9 @@
         wait(rrs.at[pl.ds(0, 4)], "r_rs", send)
 
 
-def final_kernel(a, p, li, m, s, ut, u, pc, out, xx, e):
+def final_kernel(a, p, nu, li, m, s, ut, u, pc, out, band, xx, e, save):
+    top = pltpu.make_async_copy(nu, band, save.at[4])
+    top.start()
     r, c = lax.axis_index("row"), lax.axis_index("col")
     eye = (
         lax.broadcasted_iota(jnp.int32, (512, 512), 0)
@@ -562,9 +569,16 @@
     inv = xx[...] + dot3(xs, rest, 1, 0)
     nis = split(dot3(inv, li[...], 1, 0))
     yts = split(jnp.where(c == 0, eye, dot3(nis, pc[...], 1, 1)))
-    zt = ut[...] - dot3(s[...], yts, 1, 0)
-    y = jnp.where(r == 0, eye, dot3(p[...], nis, 1, 1))
-    out[...] = a[...] - dot3(y, zt, 1, 0) - dot3(u[...], yts, 1, 0)
+    zts = split(ut[...] - dot3(s[...], yts, 1, 0))
+    xx[...] = jnp.where(r == 0, eye, dot3(p[...], nis, 1, 1))
+    saves = []
+    for q in range(4):
+        part = pl.ds(128 * q, 128)
+        e[part] = a[part] - dot3(xx[part], zts, 1, 0) - dot3(u[part], yts, 1, 0)
+        saves.append(pltpu.make_async_copy(e.at[part], out.at[part], save.at[q]))
+        saves[-1].start()
+    for copy in [top, *saves]:
+        copy.wait()
 
 
 def solution(mesh):
@@ -572,6 +586,7 @@
     nx = {4: 2, 16: 4}[n]
     zc, rr = n // 2, 128 // n
     vm = pl.BlockSpec(memory_space=pltpu.VMEM)
+    hbm = pl.BlockSpec(memory_space=pltpu.HBM)
     sq = jax.ShapeDtypeStruct((512, 512), F32)
     shape = (2, nx, nx, 2, rr, 512)
 
@@ -582,9 +597,12 @@
         nu, li, m, s, ut, u, pc = pl.pallas_call(
             functools.partial(main_kernel, nx),
             out_shape=[sq] * 6 + [jax.ShapeDtypeStruct(shape, F32)],
-            in_specs=[vm] * 2,
+            in_specs=[hbm] * 2,
             out_specs=[vm] * 7,
             scratch_shapes=[
+                scratch(*shape[:-1]),
+                scratch(*shape[:-1]),
+                pltpu.SemaphoreType.DMA((2,)),
                 scratch(5, *shape[:-1]),
                 scratch(*shape[:-1]),
                 scratch(*shape[:-1]),
@@ -610,17 +628,19 @@
             ],
             compiler_params=pltpu.CompilerParams(collective_id=0, has_side_effects=True, vmem_limit_bytes=34 << 20),
             name="exchange_factor",
-        )(trailing.reshape(shape), panel.reshape(shape))
-        out = pl.pallas_call(
+        )(
+            pltpu.with_memory_space_constraint(trailing.reshape(shape), pltpu.HBM),
+            pltpu.with_memory_space_constraint(panel.reshape(shape), pltpu.HBM),
+        )
+        return pl.pallas_call(
             final_kernel,
-            out_shape=sq,
-            in_specs=[vm] * 8,
-            out_specs=vm,
-            scratch_shapes=[pltpu.VMEM((512, 512), F32)] * 2,
+            out_shape=[sq, sq],
+            in_specs=[vm] * 9,
+            out_specs=[hbm] * 2,
+            scratch_shapes=[pltpu.VMEM((512, 512), F32)] * 2 + [pltpu.SemaphoreType.DMA((5,))],
             compiler_params=pltpu.CompilerParams(vmem_limit_bytes=30 << 20),
             name="update",
-        )(trailing, panel, li, m, s, ut, u, pc.reshape(512, 512))
-        return out, nu
+        )(trailing, panel, nu, li, m, s, ut, u, pc.reshape(512, 512))
 
     return jax.shard_map(
         step, mesh=mesh, in_specs=(P("row", "col"), P("row", None)),

time: 111 us -> 106 us (0.955); the launches traced: 109 us -> 106 us
  local copies, waits for them, and re-layouts: 3.42 us -> 0.01 us
    unnamed x9 -> x4, local copies, waits for them, and re-layouts: 3.42 us -> 0.01 us
where the time goes in v3:
time: 106 us
  Pallas kernels  105 us (99%)
    pallas_call x1, Pallas kernels, step(): pl.pallas_call(functools.partial(main_kernel, nx), out_shape=[sq] * 6 + [...  90.9 us
    pallas_call x1, Pallas kernels, step(): pl.pallas_call(final_kernel, out_shape=[sq, sq], in_specs=[vm] * 9, out_s...  13.9 us

profile of v3, /device:TPU:32, one launch (start us, length us, event | category | flops | bytes accessed | tf_op | source)
XLA Modules:
  0.0 105.7 jit_solution(9726851314861241132)
XLA Ops:
  0.6 0.0 copy-start
  0.6 0.0 copy-start.1
  0.6 90.9 %exchange_factor.1 = (f32[512,512]{1,0:T(8,128)S(1)}, f32[512,512]{1,0:T(8,128)S(1)}, f32[512,512]{1,0:T(8,128)S(1)}, f32[512,512]{1,0:T(8,128)S(1)}, f32[512,51...) custom-call(f32[2,4,4,2,8,512]{5,4,3,2,1,0:T(8,128)} %bitcast.3, ...), custom_call_target="tpu_custom_call" | custom-call | tf_op jit(solution)/shard_map/exchange_factor/pallas_call | solution.py:597
  91.6 0.0 copy-done
  91.6 0.0 copy-done.1
  91.6 13.9 %update.1 = (f32[512,512]{1,0:T(8,128)}, f32[512,512]{1,0:T(8,128)}) custom-call(f32[512,512]{1,0:T(8,128)S(1)} %copy-done, f32[512,512]{1,0:T(8,128)S(1)} %copy-done.1, f32[512,512]{1,0:T(8,128)S(1)} %get-tuple-element.9.nu, f32[512,512]{1,0:T(8,128)S(1)} %get-tuple-element.10.li, f32[512,512]{1,0:T(8,128)S(1)} %get-tuple-element.11.m, ...), custom_call_target="tpu_custom_call" | custom-call | tf_op jit(solution)/shard_map/update/pallas_call | solution.py:635
Async XLA Ops:
  0.6 90.9 %copy-start = (f32[512,512]{1,0:T(8,128)S(1)}, f32[512,512]{1,0:T(8,128)}, u32[]{:S(2)}) copy-start(f32[512,512]{1,0:T(8,128)} %a.1) | copy-start | bytes 3145732
  0.6 90.9 %copy-start.1 = (f32[512,512]{1,0:T(8,128)S(1)}, f32[512,512]{1,0:T(8,128)}, u32[]{:S(2)}) copy-start(f32[512,512]{1,0:T(8,128)} %p.1) | copy-start | bytes 3145732

commit v4 on v3

--- a/solution.py
+++ b/solution.py
@@ -30,6 +30,18 @@
     dims = (((ca,), (cb,)), ((), ()))
     d = functools.partial(lax.dot_general, dimension_numbers=dims, preferred_element_type=F32)
     return d(ah, bh) + (d(ah, bl) + d(al, bh))
+
+
+def lower_times(lower, x, cb):
+    xs = split(x)
+    head = tuple(v[:256] if cb == 0 else v[:, :256] for v in xs)
+    return jnp.concatenate([dot3(lower[0], head, 1, cb), dot3(lower[1], xs, 1, cb)], axis=0)
+
+
+def times_upper(x, lower):
+    xs = split(x)
+    head = tuple(v[:, :256] for v in xs)
+    return jnp.concatenate([dot3(head, lower[0], 1, 1), dot3(xs, lower[1], 1, 1)], axis=1)
 
 
 def bc(x):
@@ -476,22 +488,22 @@
         lax.broadcasted_iota(jnp.int32, (512, 512), 0)
         == lax.broadcasted_iota(jnp.int32, (512, 512), 1)
     ).astype(F32)
-    lis = split(li[...])
+    lis = split(li[:256, :256]), split(li[256:, :])
     half_end(P0)
-    m[...] = eye + dot3(lis, cm[P0].reshape(512, 512), 1, 1)
+    m[...] = eye + lower_times(lis, cm[P0].reshape(512, 512), 1)
     full(a0c, "a0", steps)
     full(bct, "bc", steps)
-    ut[...] = dot3(lis, whole(bct), 1, 0) + whole(a0c)
+    ut[...] = lower_times(lis, whole(bct), 0) + whole(a0c)
     br_swap()
     half_end(B0)
     half_end(F0)
-    s[...] = dot3(lis, cm[B0].reshape(512, 512), 1, 0)
+    s[...] = lower_times(lis, cm[B0].reshape(512, 512), 0)
     s[...] += s[...].T + cm[F0].reshape(512, 512)
     half_end(R)
-    s[...] += dot3(lis, dot3(cm[R].reshape(512, 512), lis, 1, 1), 1, 0)
+    s[...] += lower_times(lis, times_upper(cm[R].reshape(512, 512), lis), 0)
     wait(br.at[1 - k], "br_w")
     wait(fr.at[1 - k], "fr_w")
-    u[...] = dot3(whole(br), lis, 1, 1) + whole(fr)
+    u[...] = times_upper(whole(br), lis) + whole(fr)
 
     scattered = grs.at[pl.ds(0, n - 1)]
 
@@ -553,7 +565,7 @@
 
     def more(state):
         step, now = state
-        return jnp.logical_and(step < 48, now > 1e-3)
+        return jnp.logical_and(step < 48, now > 0.1)
 
     def square(state):
         step, _ = state
@@ -564,10 +576,26 @@
         return step + 1, jnp.sum(ee * ee)
 
     lax.while_loop(more, square, (jnp.int32(0), jnp.float32(1.0)))
+
+    ms = split(m[...])
+
+    def rough(state):
+        step, now = state
+        return jnp.logical_and(step < 5, now > 1e-5)
+
+    def newton(state):
+        step, _ = state
+        xs = split(xx[...])
+        rest = eye - dot3(ms, xs, 1, 0)
+        xx[...] += dot3(xs, rest, 1, 0)
+        return step + 1, jnp.sum(rest * rest)
+
+    lax.while_loop(rough, newton, (jnp.int32(0), jnp.float32(1.0)))
     xs = split(xx[...])
-    rest = eye - dot3(m[...], xs, 1, 0)
-    inv = xx[...] + dot3(xs, rest, 1, 0)
-    nis = split(dot3(inv, li[...], 1, 0))
+    tail = tuple(v[:, 256:] for v in xs)
+    nis = split(jnp.concatenate(
+        [dot3(xs, li[:, :256], 1, 0), dot3(tail, li[256:, 256:], 1, 0)], axis=1
+    ))
     yts = split(jnp.where(c == 0, eye, dot3(nis, pc[...], 1, 1)))
     zts = split(ut[...] - dot3(s[...], yts, 1, 0))
     xx[...] = jnp.where(r == 0, eye, dot3(p[...], nis, 1, 1))

time: 106 us -> 105 us (level)
  no operation moved by 1% of the time
where the time goes in v4:
time: 105 us; the launch traced here: 104 us
  Pallas kernels  104 us (99%)
    pallas_call x1, Pallas kernels, step(): pl.pallas_call(functools.partial(main_kernel, nx), out_shape=[sq] * 6 + [...  90.1 us
    pallas_call x1, Pallas kernels, step(): pl.pallas_call(final_kernel, out_shape=[sq, sq], in_specs=[vm] * 9, out_s...  13.5 us

profile of v4, /device:TPU:32, one launch (start us, length us, event | category | flops | bytes accessed | tf_op | source)
XLA Modules:
  0.0 104.5 jit_solution(6128509252231386342)
XLA Ops:
  0.6 0.0 copy-start
  0.6 0.0 copy-start.1
  0.6 90.1 %exchange_factor.1 = (f32[512,512]{1,0:T(8,128)S(1)}, f32[512,512]{1,0:T(8,128)S(1)}, f32[512,512]{1,0:T(8,128)S(1)}, f32[512,512]{1,0:T(8,128)S(1)}, f32[512,51...) custom-call(f32[2,4,4,2,8,512]{5,4,3,2,1,0:T(8,128)} %bitcast.3, ...), custom_call_target="tpu_custom_call" | custom-call | tf_op jit(solution)/shard_map/exchange_factor/pallas_call | solution.py:625
  90.8 0.0 copy-done
  90.8 0.0 copy-done.1
  90.8 13.5 %update.1 = (f32[512,512]{1,0:T(8,128)}, f32[512,512]{1,0:T(8,128)}) custom-call(f32[512,512]{1,0:T(8,128)S(1)} %copy-done, f32[512,512]{1,0:T(8,128)S(1)} %copy-done.1, f32[512,512]{1,0:T(8,128)S(1)} %get-tuple-element.9.nu, f32[512,512]{1,0:T(8,128)S(1)} %get-tuple-element.10.li, f32[512,512]{1,0:T(8,128)S(1)} %get-tuple-element.11.m, ...), custom_call_target="tpu_custom_call" | custom-call | tf_op jit(solution)/shard_map/update/pallas_call | solution.py:663
Async XLA Ops:
  0.6 90.1 %copy-start = (f32[512,512]{1,0:T(8,128)S(1)}, f32[512,512]{1,0:T(8,128)}, u32[]{:S(2)}) copy-start(f32[512,512]{1,0:T(8,128)} %a.1) | copy-start | bytes 3145732
  0.6 90.1 %copy-start.1 = (f32[512,512]{1,0:T(8,128)S(1)}, f32[512,512]{1,0:T(8,128)}, u32[]{:S(2)}) copy-start(f32[512,512]{1,0:T(8,128)} %p.1) | copy-start | bytes 3145732

commit v5 on v4

--- a/solution.py
+++ b/solution.py
@@ -445,13 +445,13 @@
     before = [
         g(G, 0), pc_start, spread_a0(0), g(G, 1), b_step(1), fr_start, spread_a0(1),
         g(G, 2), f(pc, "pc", 1), b_step(2), spread_a0(2), g(G, 3), f(pc, "pc", 2), b_step(3),
-        spread_a0(3), g(G, 4), f(pc, "pc", 3), b_done, spread_a0(4), spread_p0,
+        g(G, 4), f(pc, "pc", 3), b_done, spread_a0(3),
     ]
     for action in before:
         action()
 
     hooks = [
-        [],
+        [spread_a0(4), spread_p0],
         [bq_start],
         [rp_start, f(bct, "bc", 1), a0_start],
         [br_reduce, f(bct, "bc", 2), p0_start, b0_start],

time: 105 us -> 107 us (1.019)
  Pallas kernels: 104 us -> 106 us
    pallas_call x1, Pallas kernels: 90.1 us -> 92.7 us  [step(): pl.pallas_call(functools.partial(main_kernel, nx), out_shape=[sq] * 6 + [...]
where the time goes in v5:
time: 107 us
  Pallas kernels  106 us (99%)
    pallas_call x1, Pallas kernels, step(): pl.pallas_call(functools.partial(main_kernel, nx), out_shape=[sq] * 6 + [...  92.7 us
    pallas_call x1, Pallas kernels, step(): pl.pallas_call(final_kernel, out_shape=[sq, sq], in_specs=[vm] * 9, out_s...  13.6 us

profile of v5, /device:TPU:32, one launch (start us, length us, event | category | flops | bytes accessed | tf_op | source)
XLA Modules:
  0.0 107.1 jit_solution(9078830158172000675)
XLA Ops:
  0.6 0.0 copy-start
  0.6 0.0 copy-start.1
  0.6 92.7 %exchange_factor.1 = (f32[512,512]{1,0:T(8,128)S(1)}, f32[512,512]{1,0:T(8,128)S(1)}, f32[512,512]{1,0:T(8,128)S(1)}, f32[512,512]{1,0:T(8,128)S(1)}, f32[512,51...) custom-call(f32[2,4,4,2,8,512]{5,4,3,2,1,0:T(8,128)} %bitcast.3, ...), custom_call_target="tpu_custom_call" | custom-call | tf_op jit(solution)/shard_map/exchange_factor/pallas_call | solution.py:625
  93.3 0.0 copy-done
  93.3 0.0 copy-done.1
  93.3 13.6 %update.1 = (f32[512,512]{1,0:T(8,128)}, f32[512,512]{1,0:T(8,128)}) custom-call(f32[512,512]{1,0:T(8,128)S(1)} %copy-done, f32[512,512]{1,0:T(8,128)S(1)} %copy-done.1, f32[512,512]{1,0:T(8,128)S(1)} %get-tuple-element.9.nu, f32[512,512]{1,0:T(8,128)S(1)} %get-tuple-element.10.li, f32[512,512]{1,0:T(8,128)S(1)} %get-tuple-element.11.m, ...), custom_call_target="tpu_custom_call" | custom-call | tf_op jit(solution)/shard_map/update/pallas_call | solution.py:663
Async XLA Ops:
  0.6 92.7 %copy-start = (f32[512,512]{1,0:T(8,128)S(1)}, f32[512,512]{1,0:T(8,128)}, u32[]{:S(2)}) copy-start(f32[512,512]{1,0:T(8,128)} %a.1) | copy-start | bytes 3145732
  0.6 92.7 %copy-start.1 = (f32[512,512]{1,0:T(8,128)S(1)}, f32[512,512]{1,0:T(8,128)}, u32[]{:S(2)}) copy-start(f32[512,512]{1,0:T(8,128)} %p.1) | copy-start | bytes 3145732
